TPU v7x, 32 devices: a whole 2x2x4 slice. The times are simulated.
32 devices in a mesh: dp: 4 (over y, x), expert: 8 (over z, core).
Axes of the slice: x: 2, y: 2, z: 4, core: 2. Of those that a mesh axis runs over, the one named last changes fastest.
Arguments:
- tokens: bfloat16 [1024, 2048], P(('dp', 'expert')), may hold values from -6 to 6
- grad_out: bfloat16 [1024, 2048], P(('dp', 'expert')), may hold values from -0.59765625 to 0.59765625
- routing: int32 [1024, 8], P(('dp', 'expert')), may hold values from 0 to 15, as said below
- replica: int32 [1024, 8], P(('dp', 'expert')), may hold values from 0 to 1, as said below
- gates: bfloat16 [1024, 8], P(('dp', 'expert')), may hold values from 0.25 to 4
- host_expert: int32 [8], replicated, may hold values from 0 to 15, as said below
- w_gate_up: bfloat16 [16, 2, 768, 2048], P('expert', None, 'dp'), may hold values from -0.125 to 0.125
- w_down: bfloat16 [16, 768, 2048], P('expert', 'dp'), may hold values from -0.21875 to 0.21875
Outputs:
- grad_tokens: bfloat16 [1024, 2048], P(('dp', 'expert'))
- grad_gates: float32 [1024, 8], P(('dp', 'expert'))
- grad_w_gate_up: bfloat16 [16, 2, 768, 2048], P('expert', None, 'dp')
- grad_w_down: bfloat16 [16, 768, 2048], P('expert', 'dp')
Inputs may be any that keep to these rules, and one draw needn't show every extreme that they name: `routing`: column k of a token names an expert of 2 * k to 2 * k + 1. Within the rows of one device, experts 2 i and 2 i + 1 are named together exactly 2 * 16 times. `replica`: within the rows of one device, each expert has at most 16 choices marked 0 and at most 16 marked 1; some expert reaches 16 marked 0 from every device, and in every index of dp some expert reaches 16 marked 1 from every device. Only experts listed in host_expert have choices marked 1. `host_expert`: for every device d of the expert axis exactly one of its experts 2 d and 2 d + 1 is listed, and it is listed once.
All inputs are finite; a program needn't handle non-finite values.
Results may differ from a plain program's by a relative error of at most 0.013.
Values may be sent and summed in bfloat16 or wider, within the bound.
A program may use at most 128 MiB of HBM per device.

v0:
```python
import jax
import jax.numpy as jnp
from jax import lax
from jax.sharding import PartitionSpec as P


def lookup(values_table, indices):
    matches = indices[..., None] == lax.broadcasted_iota(
        jnp.int32, indices.shape + values_table.shape, indices.ndim
    )
    return jnp.sum(jnp.where(matches, values_table, 0), axis=-1)


def placement(host_expert, owned_experts, devices):
    experts = owned_experts * devices
    matches = host_expert[None, :] == lax.broadcasted_iota(jnp.int32, (experts, devices), 0)
    helper_ids = lax.broadcasted_iota(jnp.int32, (experts, devices), 1)
    helper_of = jnp.sum(jnp.where(matches, helper_ids, 0), axis=1)
    listed = jnp.sum(matches.astype(jnp.int32), axis=1)
    return (helper_of, listed)


def targets(routing, replica, host_expert, owned_experts, devices, slot_rows, groups):
    helper_of, listed = placement(host_expert, owned_experts, devices)
    choices = routing.shape[0] // groups * routing.shape[1]
    usable = (replica == 0) | (lookup(listed, routing) > 0)
    device_to = jnp.where(replica == 0, routing // owned_experts, lookup(helper_of, routing))
    block_to = jnp.where(replica == 0, routing % owned_experts, owned_experts)
    labels = (routing * 2 + replica).reshape(groups, choices)
    earlier = lax.broadcasted_iota(jnp.int32, (choices, choices), 1) < lax.broadcasted_iota(
        jnp.int32, (choices, choices), 0
    )
    matching = (labels[:, :, None] == labels[:, None, :]) & earlier[None]
    ranking = jnp.sum(matching.astype(jnp.int32), axis=2).reshape(routing.shape)
    group_ids = lax.broadcasted_iota(jnp.int32, (groups, choices), 0).reshape(routing.shape)
    position = ((block_to * groups + group_ids) * devices + device_to) * slot_rows + ranking
    return jnp.where(usable, position, -1)


def selector(position, total_slots):
    matches = position[None, :, :] == lax.broadcasted_iota(
        jnp.int32, (total_slots,) + position.shape, 0
    )
    picker = jnp.sum(matches.astype(jnp.float32), axis=2).astype(jnp.bfloat16)
    return (matches, picker)


def fill_rows(matches, picker, tokens, grad_out, gates):
    row_x = jnp.dot(picker, tokens, preferred_element_type=jnp.float32).astype(jnp.bfloat16)
    row_dy = jnp.dot(picker, grad_out, preferred_element_type=jnp.float32).astype(jnp.bfloat16)
    row_gate = jnp.sum(
        jnp.where(matches, gates[None].astype(jnp.float32), 0.0), axis=(1, 2)
    ).astype(jnp.bfloat16)
    return (row_x, row_dy, row_gate)


def expert_block(inputs, upstream, weight, gate_up, down_matrix):
    mixed = jnp.einsum("rd,jfd->jrf", inputs, gate_up, preferred_element_type=jnp.float32)
    gate_pre = mixed[0]
    up_part = mixed[1]
    sigmoid_gate = jax.nn.sigmoid(gate_pre)
    active = gate_pre * sigmoid_gate
    hidden = (active * up_part).astype(jnp.bfloat16)
    output_part = jnp.einsum("rf,fd->rd", hidden, down_matrix, preferred_element_type=jnp.float32)
    gate_part = jnp.sum(output_part * upstream.astype(jnp.float32), axis=1)
    scaled = (weight.astype(jnp.float32)[:, None] * upstream.astype(jnp.float32)).astype(
        jnp.bfloat16
    )
    grad_hidden = jnp.einsum("rd,fd->rf", scaled, down_matrix, preferred_element_type=jnp.float32)
    grad_gate = grad_hidden * up_part * sigmoid_gate * (1.0 + gate_pre * (1.0 - sigmoid_gate))
    grad_mixed = jnp.stack([grad_gate, grad_hidden * active], axis=0).astype(jnp.bfloat16)
    input_part = jnp.einsum("jrf,jfd->rd", grad_mixed, gate_up, preferred_element_type=jnp.float32)
    weight_gu = jnp.einsum("jrf,rd->jfd", grad_mixed, inputs, preferred_element_type=jnp.float32)
    weight_down = jnp.einsum("rf,rd->fd", hidden, scaled, preferred_element_type=jnp.float32)
    return (input_part, gate_part, weight_gu, weight_down)


def shards(tokens, grad_out, routing, replica, gates, host_expert, w_gate_up, w_down):
    devices = lax.axis_size("expert")
    device_id = lax.axis_index("expert")
    token_rows, features = tokens.shape
    owned_experts = w_gate_up.shape[0]
    quarter = w_down.shape[1]
    topk_width = routing.shape[1]
    slot_rows = token_rows * topk_width // (owned_experts * devices)
    blocks = owned_experts + 1
    lane_rows = devices * slot_rows
    piece_rows = quarter // devices
    home_slots = targets(routing, replica, host_expert, owned_experts, devices, slot_rows, 1)
    home_matches, home_picker = selector(home_slots, blocks * lane_rows)
    row_x, row_dy, row_gate = fill_rows(home_matches, home_picker, tokens, grad_out, gates)
    sent_x, sent_dy, sent_gate = (
        lax.all_to_all(
            row_x.reshape(blocks, lane_rows, features),
            "expert",
            split_axis=1,
            concat_axis=1,
            tiled=True,
        ),
        lax.all_to_all(
            row_dy.reshape(blocks, lane_rows, features),
            "expert",
            split_axis=1,
            concat_axis=1,
            tiled=True,
        ),
        lax.all_to_all(
            row_gate.reshape(blocks, lane_rows), "expert", split_axis=1, concat_axis=1, tiled=True
        ),
    )
    block_x, block_dy, block_gate = (
        lax.all_gather(sent_x, "dp", axis=1, tiled=True),
        lax.all_gather(sent_dy, "dp", axis=1, tiled=True),
        lax.all_gather(sent_gate, "dp", axis=1, tiled=True),
    )
    owner_of_helper = host_expert // owned_experts
    owns_copy = owner_of_helper == device_id
    copied_local = jnp.sum(jnp.where(owns_copy, host_expert % owned_experts, 0))
    helper_ids = lax.broadcasted_iota(jnp.int32, (devices, devices), 1)
    owner_ids = lax.broadcasted_iota(jnp.int32, (devices, devices), 0)
    helper_of_owner = jnp.sum(
        jnp.where(owner_of_helper[None, :] == owner_ids, helper_ids, 0), axis=1
    )
    source_gu = lax.dynamic_index_in_dim(w_gate_up, copied_local, 0, keepdims=False)
    source_down = lax.dynamic_index_in_dim(w_down, copied_local, 0, keepdims=False)
    spread_gu, spread_down = (
        lax.all_to_all(
            source_gu.reshape(2, devices, piece_rows, features),
            "expert",
            split_axis=1,
            concat_axis=1,
            tiled=True,
        ),
        lax.all_to_all(
            source_down.reshape(1, devices, piece_rows, features),
            "expert",
            split_axis=1,
            concat_axis=1,
            tiled=True,
        ),
    )
    spread_gu = jnp.take(spread_gu, owner_of_helper, axis=1)
    spread_down = jnp.take(spread_down, owner_of_helper, axis=1)
    hosted_gu, hosted_down = (
        lax.all_to_all(spread_gu, "expert", split_axis=1, concat_axis=1, tiled=True),
        lax.all_to_all(spread_down, "expert", split_axis=1, concat_axis=1, tiled=True),
    )
    hosted_gu = hosted_gu.reshape(2, quarter, features)
    hosted_down = hosted_down.reshape(quarter, features)
    input_parts = []
    gate_parts = []
    owner_gu = []
    owner_down = []
    for block in range(blocks):
        if block < owned_experts:
            gate_up = w_gate_up[block]
            down_matrix = w_down[block]
        else:
            gate_up = hosted_gu
            down_matrix = hosted_down
        input_part, gate_part, weight_gu, weight_down = expert_block(
            block_x[block], block_dy[block], block_gate[block], gate_up, down_matrix
        )
        input_parts.append(input_part.astype(jnp.bfloat16))
        gate_parts.append(gate_part.astype(jnp.bfloat16))
        owner_gu.append(weight_gu)
        owner_down.append(weight_down)
    helper_gu = owner_gu[owned_experts].astype(jnp.bfloat16)
    helper_down = owner_down[owned_experts].astype(jnp.bfloat16)
    back_gu, back_down = (
        lax.all_to_all(
            helper_gu.reshape(2, devices, piece_rows, features),
            "expert",
            split_axis=1,
            concat_axis=1,
            tiled=True,
        ),
        lax.all_to_all(
            helper_down.reshape(1, devices, piece_rows, features),
            "expert",
            split_axis=1,
            concat_axis=1,
            tiled=True,
        ),
    )
    back_gu = jnp.take(back_gu, helper_of_owner, axis=1)
    back_down = jnp.take(back_down, helper_of_owner, axis=1)
    extra_gu, extra_down = (
        lax.all_to_all(back_gu, "expert", split_axis=1, concat_axis=1, tiled=True),
        lax.all_to_all(back_down, "expert", split_axis=1, concat_axis=1, tiled=True),
    )
    extra_gu = extra_gu.reshape(2, quarter, features).astype(jnp.float32)
    extra_down = extra_down.reshape(quarter, features).astype(jnp.float32)
    stacked_dx = jnp.stack(input_parts, axis=0)
    stacked_dg = jnp.stack(gate_parts, axis=0)
    summed_dx, summed_dg = (
        lax.psum_scatter(stacked_dx, "dp", scatter_dimension=1, tiled=True).astype(jnp.float32),
        lax.psum_scatter(stacked_dg, "dp", scatter_dimension=1, tiled=True).astype(jnp.float32),
    )
    row_dx = summed_dx.astype(jnp.bfloat16)
    row_dg = summed_dg.astype(jnp.bfloat16)
    home_dx, home_dg = (
        lax.all_to_all(row_dx, "expert", split_axis=1, concat_axis=1, tiled=True),
        lax.all_to_all(row_dg, "expert", split_axis=1, concat_axis=1, tiled=True),
    )
    home_dx = home_dx.reshape(blocks * lane_rows, features)
    home_dg = home_dg.reshape(blocks * lane_rows).astype(jnp.float32)
    grad_tokens = jnp.einsum(
        "st,sd->td", home_picker, home_dx, preferred_element_type=jnp.float32
    ).astype(jnp.bfloat16)
    grad_gates = jnp.sum(jnp.where(home_matches, home_dg[:, None, None], 0.0), axis=0)
    grad_gu = []
    grad_down = []
    for block in range(owned_experts):
        present = (copied_local == block).astype(jnp.float32)
        grad_gu.append((owner_gu[block] + present * extra_gu).astype(jnp.bfloat16))
        grad_down.append((owner_down[block] + present * extra_down).astype(jnp.bfloat16))
    return (grad_tokens, grad_gates, jnp.stack(grad_gu, axis=0), jnp.stack(grad_down, axis=0))


def solution(mesh):
    in_specs = (
        P(("dp", "expert"), None),
        P(("dp", "expert"), None),
        P(("dp", "expert"), None),
        P(("dp", "expert"), None),
        P(("dp", "expert"), None),
        P(),
        P("expert", None, "dp", None),
        P("expert", "dp", None),
    )
    out_specs = (
        P(("dp", "expert"), None),
        P(("dp", "expert"), None),
        P("expert", None, "dp", None),
        P("expert", "dp", None),
    )
    return jax.shard_map(shards, mesh=mesh, in_specs=in_specs, out_specs=out_specs, check_vma=False)
```

profile of v0, /device:TPU:0, one launch (start us, length us, event | category | flops | bytes accessed | tf_op | source)
XLA Modules:
  0.0 546.3 jit_solution(6755420541427667318)
XLA Ops:
  11.6 1.4 copy.113
  13.0 55.2 %all_to_all.73 = bf16[3,128,2048]{2,0,1:T(4,128)(2,1)S(1)} all-to-all(bf16[3,128,2048]{2,0,1:T(4,128)(2,1)S(1)} %copy.113), channel_id=1, replica_groups=mesh['dp'=4,'expert'=8] {'expert'}, dimensions={1} | all-to-all | bytes 3145728 | tf_op jit(solution)/shard_map/all_to_all | solution.py:93
  68.2 2.3 copy.114
  71.1 1.4 copy.111
  72.5 51.5 %all_to_all.74 = bf16[3,128,2048]{2,0,1:T(4,128)(2,1)S(1)} all-to-all(bf16[3,128,2048]{2,0,1:T(4,128)(2,1)S(1)} %copy.111), channel_id=1, replica_groups=mesh['dp'=4,'expert'=8] {'expert'}, dimensions={1} | all-to-all | bytes 3145728 | tf_op jit(solution)/shard_map/all_to_all | solution.py:100
  124.0 2.3 copy.112
  129.1 1.3 copy.116
  130.4 3.7 all-to-all-start.5
  135.1 36.7 %all-to-all-done.5 = bf16[2,8,24,2048]{3,2,0,1:T(8,128)(2,1)S(1)} async-done(((bf16[2,8,24,2048]{3,2,0,1:T(8,128)(2,1)}), bf16[2,8,24,2048]{3,2,0,1:T(8,128)(2,1)S(1)}, u32[]{:S(2)}, u32[]{:S(2)}) %all-to-all-start.5) | async-done | bytes 1572896 | tf_op jit(solution)/shard_map/all_to_all | solution.py:127
  171.8 4.2 all-to-all-start.3
  176.9 1.4 select_bitcast_fusion.1
  178.2 18.7 %all-to-all-done.3 = bf16[1,8,24,2048]{3,2,0,1:T(8,128)(2,1)} async-done(((bf16[1,8,24,2048]{3,2,0,1:T(8,128)(2,1)}), bf16[1,8,24,2048]{3,2,0,1:T(8,128)(2,1)}, u32[]{:S(2)}, u32[]{:S(2)}) %all-to-all-start.3) | async-done | bytes 786464 | tf_op jit(solution)/shard_map/all_to_all | solution.py:134
  197.0 3.6 all-to-all-start.6
  200.6 1.7 gather_fusion
  202.3 1.0 fusion.42
  203.4 34.9 %all-to-all-done.6 = bf16[2,8,24,2048]{3,2,0,1:T(8,128)(2,1)S(1)} async-done(((bf16[2,8,24,2048]{3,2,0,1:T(8,128)(2,1)}), bf16[2,8,24,2048]{3,2,0,1:T(8,128)(2,1)S(1)}, u32[]{:S(2)}, u32[]{:S(2)}) %all-to-all-start.6) | async-done | bytes 1572896 | tf_op jit(solution)/shard_map/all_to_all | solution.py:145
  238.3 4.2 all-to-all-start.4
  242.9 2.6 fusion.34
  245.7 17.8 %all-to-all-done.4 = bf16[1,8,24,2048]{3,2,0,1:T(8,128)(2,1)} async-done(((bf16[1,8,24,2048]{3,2,0,1:T(8,128)(2,1)}), bf16[1,8,24,2048]{3,2,0,1:T(8,128)(2,1)}, u32[]{:S(2)}, u32[]{:S(2)}) %all-to-all-start.4) | async-done | bytes 786464 | tf_op jit(solution)/shard_map/all_to_all | solution.py:146
  263.5 2.8 fusion.8
  266.3 3.2 fusion.35
  270.6 1.1 copy-done.5
  271.7 2.6 fusion.38
  275.9 1.5 copy.130
  277.4 23.2 %reduce-scatter.7.cloned.1.call-done = bf16[128,3]{1,0:T(8,128)(2,1)} async-done(((bf16[512,3]{1,0:T(8,128)(2,1)}), bf16[128,3]{1,0:T(8,128)(2,1)}) %reduce-scatter.7.cloned.1.call-update) | async-done | bytes 784
  300.7 1.5 copy.121
  302.1 4.6 all-to-all-start.8
  306.8 1.4 copy.108
  308.1 4.0 all-to-all-done.8
  312.1 1.3 copy_convert_fusion
  313.4 1.4 reshape.297
  314.8 1.5 select_reduce_fusion
  317.0 8.0 %all_to_all.75 = bf16[3,8,16]{2,0,1:T(4,128)(2,1)S(1)} all-to-all(bf16[3,8,16]{2,0,1:T(4,128)(2,1)S(1)} %copy.109), channel_id=1, replica_groups=mesh['dp'=4,'expert'=8] {'expert'}, dimensions={1} | all-to-all | bytes 1536 | tf_op jit(solution)/shard_map/all_to_all | solution.py:107
  325.1 8.2 %all_gather.9 = bf16[3,512]{1,0:T(4,128)(2,1)S(1)} all-gather(bf16[3,128]{1,0:T(4,128)(2,1)S(1)} %all_to_all.46), channel_id=1, replica_groups=mesh['dp'=4,'expert'=8] {'dp'}, dimensions={1}, use_global_device_ids=true | all-gather | bytes 3840 | tf_op jit(solution)/shard_map/all_gather | solution.py:114
  333.4 2.9 fusion.99
  336.4 1.3 fusion.13
  338.7 1.0 fusion.98
  340.6 1.3 fusion.12
  341.9 1.0 fusion.97
  343.0 1.3 fusion.11
  344.3 3.2 pad_maximum_fusion
  348.5 3.2 convolution_convert_fusion.3
  351.7 3.5 all-to-all-start.11
  355.3 2.6 convolution_convert_fusion.2
  357.8 1.2 copy.123
  359.1 17.0 %all-to-all-done.11 = bf16[1,8,24,2048]{3,2,0,1:T(8,128)(2,1)S(1)} async-done(((bf16[1,8,24,2048]{3,2,0,1:T(8,128)(2,1)}), bf16[1,8,24,2048]{3,2,0,1:T(8,128)(2,1)S(1)}, u32[]{:S(2)}, u32[]{:S(2)}) %all-to-all-start.11) | async-done | bytes 786464 | tf_op jit(solution)/shard_map/all_to_all | solution.py:178
  376.1 3.6 all-to-all-start.9
  381.5 35.9 %all-to-all-done.9 = bf16[2,8,24,2048]{3,2,0,1:T(8,128)(2,1)S(1)} async-done(((bf16[2,8,24,2048]{3,2,0,1:T(8,128)(2,1)}), bf16[2,8,24,2048]{3,2,0,1:T(8,128)(2,1)S(1)}, u32[]{:S(2)}, u32[]{:S(2)}) %all-to-all-start.9) | async-done | bytes 1572896 | tf_op jit(solution)/shard_map/all_to_all | solution.py:171
  417.4 4.2 all-to-all-start.12
  422.5 1.4 select_bitcast_fusion
  423.8 18.8 %all-to-all-done.12 = bf16[1,8,24,2048]{3,2,0,1:T(8,128)(2,1)} async-done(((bf16[1,8,24,2048]{3,2,0,1:T(8,128)(2,1)}), bf16[1,8,24,2048]{3,2,0,1:T(8,128)(2,1)}, u32[]{:S(2)}, u32[]{:S(2)}) %all-to-all-start.12) | async-done | bytes 786464 | tf_op jit(solution)/shard_map/all_to_all | solution.py:190
  442.6 3.6 all-to-all-start.10
  448.1 4.1 copy.119
  452.2 31.7 %all-to-all-done.10 = bf16[2,8,24,2048]{3,2,0,1:T(8,128)(2,1)S(1)} async-done(((bf16[2,8,24,2048]{3,2,0,1:T(8,128)(2,1)}), bf16[2,8,24,2048]{3,2,0,1:T(8,128)(2,1)S(1)}, u32[]{:S(2)}, u32[]{:S(2)}) %all-to-all-start.10) | async-done | bytes 1572896 | tf_op jit(solution)/shard_map/all_to_all | solution.py:189
  483.9 1.1 copy-done.2
  485.0 3.9 all-to-all-start.7
  488.9 1.5 convert_multiply_fusion.6
  490.4 2.3 fusion.18
  492.8 2.3 fusion.19
  495.1 1.3 pad_maximum_fusion.2
  502.2 1.9 pad_maximum_fusion.1
  504.2 33.4 %all-to-all-done.7 = bf16[3,128,2048]{2,0,1:T(4,128)(2,1)S(1)} async-done(((bf16[3,128,2048]{2,0,1:T(4,128)(2,1)}), bf16[3,128,2048]{2,0,1:T(4,128)(2,1)S(1)}, u32[]{:S(2)}, u32[]{:S(2)}) %all-to-all-start.7) | async-done | bytes 1572896 | tf_op jit(solution)/shard_map/all_to_all | solution.py:203
  537.6 1.1 copy.120
  538.8 1.0 convolution_convert_fusion.4
  (139 shorter events, 23.5 us)
Async XLA Ops:
  7.2 3.9 copy-start
  7.2 235.8 %all-gather.5.cloned.1.call-start = ((), (), s32[]{:S(2)}) async-start(), calls=%async_computation.16 | async-start | bytes 7864320 | tf_op jit(solution)/shard_map/all_gather | solution.py:112
  11.0 59.5 %copy-start.12 = (bf16[384,32]{0,1:T(8,128)(2,1)}, bf16[384,32]{0,1:T(8,128)(2,1)S(1)}, u32[]{:S(2)}) copy-start(bf16[384,32]{0,1:T(8,128)(2,1)S(1)} %convert_reduce_fusion) | copy-start | bytes 73732
  68.2 2.4 copy-start.24
  70.5 193.0 %all-gather.3.cloned.1.call-start = ((), (), s32[]{:S(2)}) async-start(), calls=%async_computation.15 | async-start | bytes 7864320 | tf_op jit(solution)/shard_map/all_gather | solution.py:113
  124.0 2.3 copy-start.26
  124.0 4.9 copy-start.4
  126.3 4.0 copy-start.27
  130.4 3.7 copy-start.9
  130.4 41.4 %all-to-all-start.5 = ((bf16[2,8,24,2048]{3,2,0,1:T(8,128)(2,1)}), bf16[2,8,24,2048]{3,2,0,1:T(8,128)(2,1)S(1)}, u32[]{:S(2)}, u32[]{:S(2)}) async-start(bf16[2,8,24,2048]{3,2,0,1:T(8,128)(2,1)} %copy.116), calls=%async_computation.5 | async-start | bytes 3145728 | tf_op jit(solution)/shard_map/all_to_all | solution.py:127
  171.8 25.2 %all-to-all-start.3 = ((bf16[1,8,24,2048]{3,2,0,1:T(8,128)(2,1)}), bf16[1,8,24,2048]{3,2,0,1:T(8,128)(2,1)}, u32[]{:S(2)}, u32[]{:S(2)}) async-start(bf16[1,8,24,2048]{3,2,0,1:T(8,128)(2,1)} %bitcast.30), calls=%async_computation.3 | async-start | bytes 1572864 | tf_op jit(solution)/shard_map/all_to_all | solution.py:134
  197.0 41.3 %all-to-all-start.6 = ((bf16[2,8,24,2048]{3,2,0,1:T(8,128)(2,1)}), bf16[2,8,24,2048]{3,2,0,1:T(8,128)(2,1)S(1)}, u32[]{:S(2)}, u32[]{:S(2)}) async-start(bf16[2,8,24,2048]{3,2,0,1:T(8,128)(2,1)} %select_bitcast_fusion.1), calls=%async_computation.6 | async-start | bytes 3145728 | tf_op jit(solution)/shard_map/all_to_all | solution.py:145
  238.3 25.2 %all-to-all-start.4 = ((bf16[1,8,24,2048]{3,2,0,1:T(8,128)(2,1)}), bf16[1,8,24,2048]{3,2,0,1:T(8,128)(2,1)}, u32[]{:S(2)}, u32[]{:S(2)}) async-start(bf16[1,8,24,2048]{3,2,0,1:T(8,128)(2,1)} %fusion.42), calls=%async_computation.4 | async-start | bytes 1572864 | tf_op jit(solution)/shard_map/all_to_all | solution.py:146
  242.5 58.2 %reduce-scatter.7.cloned.1.call-start = ((), (), s32[]{:S(2)}) async-start(), calls=%async_computation.18 | async-start | bytes 163840
  245.7 20.6 %copy-start.22 = (bf16[1,512,192]{1,2,0:T(8,128)(2,1)}, bf16[1,512,192]{1,2,0:T(8,128)(2,1)S(1)}, u32[]{:S(2)}) copy-start(bf16[1,512,192]{1,2,0:T(8,128)(2,1)S(1)} %multiply_convert_fusion) | copy-start | bytes 589828
  263.5 6.2 %slice-start.2 = ((s8[6291456]{0:T(1024)(128)(4,1)}), s8[4194304]{0:T(1024)(128)(4,1)S(1)}, s32[]{:S(2)}) async-start(s8[6291456]{0:T(1024)(128)(4,1)} %bitcast.321), calls=%async_computation.21 | async-start | bytes 8388608
  266.3 3.4 slice-start.3
  266.3 3.4 copy-start.10
  269.5 1.0 copy-start.7
  269.7 2.0 copy-start.5
  302.1 10.0 %all-to-all-start.8 = ((bf16[3,8,16]{2,0,1:T(4,128)(2,1)}), bf16[3,8,16]{2,0,1:T(4,128)(2,1)}, u32[]{:S(2)}, u32[]{:S(2)}) async-start(bf16[3,8,16]{2,0,1:T(4,128)(2,1)} %copy.121), calls=%async_computation.9 | async-start | bytes 16384 | tf_op jit(solution)/shard_map/all_to_all | solution.py:204
  306.7 141.4 %reduce-scatter.5.cloned.1.call-start = ((), (), s32[]{:S(2)}) async-start(), calls=%async_computation.17 | async-start | bytes 7864320 | tf_op jit(solution)/shard_map/reduce_scatter | solution.py:197
  333.4 4.3 slice-start.4
  336.3 1.4 copy-start.29
  336.3 1.4 copy-start.31
  336.3 1.8 slice-start.5
  336.3 1.9 copy-start.8
  336.4 2.4 copy-start.11
  338.7 1.9 copy-start.6
  339.8 2.1 copy-start.14
  339.8 2.1 copy-start.16
  343.0 1.3 copy-start.18
  343.0 1.3 copy-start.20
  347.5 0.9 copy-start.23
  348.5 6.8 %copy-start.30 = (bf16[1,512,192]{1,2,0:T(8,128)(2,1)S(1)}, bf16[1,512,192]{1,2,0:T(8,128)(2,1)}, u32[]{:S(2)}) copy-start(bf16[1,512,192]{1,2,0:T(8,128)(2,1)} %copy-done.29) | copy-start | bytes 589828
  348.5 6.8 %copy-start.32 = (bf16[1,512,192]{1,2,0:T(8,128)(2,1)S(1)}, bf16[1,512,192]{1,2,0:T(8,128)(2,1)}, u32[]{:S(2)}) copy-start(bf16[1,512,192]{1,2,0:T(8,128)(2,1)} %copy-done.31) | copy-start | bytes 589828
  351.7 24.4 %all-to-all-start.11 = ((bf16[1,8,24,2048]{3,2,0,1:T(8,128)(2,1)}), bf16[1,8,24,2048]{3,2,0,1:T(8,128)(2,1)S(1)}, u32[]{:S(2)}, u32[]{:S(2)}) async-start(bf16[1,8,24,2048]{3,2,0,1:T(8,128)(2,1)} %bitcast.61), calls=%async_computation.12 | async-start | bytes 1572864 | tf_op jit(solution)/shard_map/all_to_all | solution.py:178
  359.1 20.6 %copy-start.28 = (s32[8]{0:T(128)S(1)}, s32[8]{0:T(128)}, u32[]{:S(2)}) copy-start(s32[8]{0:T(128)} %copy-done.27) | copy-start | bytes 100
  376.1 41.3 %all-to-all-start.9 = ((bf16[2,8,24,2048]{3,2,0,1:T(8,128)(2,1)}), bf16[2,8,24,2048]{3,2,0,1:T(8,128)(2,1)S(1)}, u32[]{:S(2)}, u32[]{:S(2)}) async-start(bf16[2,8,24,2048]{3,2,0,1:T(8,128)(2,1)} %copy.123), calls=%async_computation.10 | async-start | bytes 3145728 | tf_op jit(solution)/shard_map/all_to_all | solution.py:171
  417.4 25.2 %all-to-all-start.12 = ((bf16[1,8,24,2048]{3,2,0,1:T(8,128)(2,1)}), bf16[1,8,24,2048]{3,2,0,1:T(8,128)(2,1)}, u32[]{:S(2)}, u32[]{:S(2)}) async-start(bf16[1,8,24,2048]{3,2,0,1:T(8,128)(2,1)} %fusion.41), calls=%async_computation.13 | async-start | bytes 1572864 | tf_op jit(solution)/shard_map/all_to_all | solution.py:190
  423.8 23.6 %copy-start.25 = (f32[32,8]{1,0:T(8,128)S(1)}, f32[32,8]{1,0:T(8,128)}, u32[]{:S(2)}) copy-start(f32[32,8]{1,0:T(8,128)} %get-tuple-element.14) | copy-start | bytes 3076
  442.6 41.3 %all-to-all-start.10 = ((bf16[2,8,24,2048]{3,2,0,1:T(8,128)(2,1)}), bf16[2,8,24,2048]{3,2,0,1:T(8,128)(2,1)S(1)}, u32[]{:S(2)}, u32[]{:S(2)}) async-start(bf16[2,8,24,2048]{3,2,0,1:T(8,128)(2,1)} %select_bitcast_fusion), calls=%async_computation.11 | async-start | bytes 3145728 | tf_op jit(solution)/shard_map/all_to_all | solution.py:189
  483.9 1.1 copy-start.2
  485.0 52.6 %all-to-all-start.7 = ((bf16[3,128,2048]{2,0,1:T(4,128)(2,1)}), bf16[3,128,2048]{2,0,1:T(4,128)(2,1)S(1)}, u32[]{:S(2)}, u32[]{:S(2)}) async-start(bf16[3,128,2048]{2,0,1:T(4,128)(2,1)} %copy.119), calls=%async_computation.8 | async-start | bytes 4194304 | tf_op jit(solution)/shard_map/all_to_all | solution.py:203
  495.1 2.0 copy-start.3
  497.1 2.2 slice-start
  497.9 2.3 slice-start.1
  498.3 1.9 copy-start.15
  498.3 1.9 copy-start.17
  500.2 1.0 copy-start.19
  500.2 1.0 copy-start.21
  502.2 37.6 %copy-start.1 = (bf16[32,2048]{1,0:T(8,128)(2,1)S(1)}, bf16[32,2048]{1,0:T(8,128)(2,1)}, u32[]{:S(2)}) copy-start(bf16[32,2048]{1,0:T(8,128)(2,1)} %param.12) | copy-start | bytes 393220
  504.2 34.6 %copy-start.13 = (bf16[384,32]{0,1:T(8,128)(2,1)S(1)}, bf16[384,32]{0,1:T(8,128)(2,1)}, u32[]{:S(2)}) copy-start(bf16[384,32]{0,1:T(8,128)(2,1)} %copy-done.12) | copy-start | bytes 73732
Sparse Core Ops, SparseCore 0:
  70.6 68.9 all-gather.4
  141.4 70.0 all-gather.2
  277.6 23.0 reduce-scatter.6
  347.7 67.2 reduce-scatter.4
where the time goes:
time: 548 us; the launch traced here: 546 us
  waiting for transfers between devices  272 us (50%)
  blocking collectives  123 us (22%)
  starting transfers between devices  39.4 us (7%)
  matrix products  36.4 us (7%)
  local copies, waits for them, and re-layouts  35.9 us (7%)
  other arithmetic  21.5 us (4%)
  between operations  17.8 us (3%)
    all_to_all x1, blocking collectives, shards(): lax.all_to_all(row_x.reshape(blocks, lane_rows, features), 'expert', spli...  55.2 us
    all_to_all x1, blocking collectives, shards(): lax.all_to_all(row_dy.reshape(blocks, lane_rows, features), 'expert', spl...  51.5 us
    all_to_all x1, waiting for transfers between devices, shards(): lax.all_to_all(source_gu.reshape(2, devices, piece_rows, features), 'expe...  36.7 us
    all_to_all x1, waiting for transfers between devices, shards(): lax.all_to_all(helper_gu.reshape(2, devices, piece_rows, features), 'expe...  35.9 us
    all_to_all x1, waiting for transfers between devices, shards(): lax.all_to_all(spread_gu, 'expert', split_axis=1, concat_axis=1, tiled=True)  34.9 us
    all_to_all x1, waiting for transfers between devices, shards(): lax.all_to_all(row_dx, 'expert', split_axis=1, concat_axis=1, tiled=True)  33.4 us
    all_to_all x1, waiting for transfers between devices, shards(): lax.all_to_all(back_gu, 'expert', split_axis=1, concat_axis=1, tiled=True)  31.7 us
    unnamed x5, waiting for transfers between devices  23.3 us
  transfers between devices with their start and end apart: 14, of which 11 were waited for; matrix products, arithmetic and copies ran while one was open for 8% of the time, Pallas kernels for 0%

commit v1 on v0

--- a/solution.py
+++ b/solution.py
@@ -200,7 +200,12 @@
     row_dx = summed_dx.astype(jnp.bfloat16)
     row_dg = summed_dg.astype(jnp.bfloat16)
     home_dx, home_dg = (
-        lax.all_to_all(row_dx, "expert", split_axis=1, concat_axis=1, tiled=True),
+        jnp.concatenate(
+            lax.all_to_all(
+                jnp.stack(jnp.split(row_dx, lax.axis_size("expert"), axis=1)), "expert", 0, 0
+            ),
+            axis=1,
+        ),
         lax.all_to_all(row_dg, "expert", split_axis=1, concat_axis=1, tiled=True),
     )
     home_dx = home_dx.reshape(blocks * lane_rows, features)

time: 548 us -> 530 us (0.967)
  waiting for transfers between devices: 272 us -> 259 us
    all_to_all x1, waiting for transfers between devices: 33.4 us -> 22.8 us  [shards(): lax.all_to_all(jnp.stack(jnp.split(row_dx, lax.axis_size('expert'), axis=...]
    unnamed x80 -> x81, local copies, waits for them, and re-layouts: 9.58 us -> 15.7 us
  transfers between devices with their start and end apart: 14 -> 14, of which waited for: 11 -> 11; matrix products, arithmetic and copies ran while one was open for 8% -> 9% of each run, Pallas kernels for 0% -> 0%
where the time goes in v1:
time: 530 us; the launch traced here: 528 us
  waiting for transfers between devices  259 us (49%)
  blocking collectives  123 us (23%)
  starting transfers between devices  39.5 us (7%)
  matrix products  36.5 us (7%)
  local copies, waits for them, and re-layouts  34.7 us (7%)
  other arithmetic  18.4 us (3%)
  between operations  17.8 us (3%)
    all_to_all x1, blocking collectives, shards(): lax.all_to_all(row_x.reshape(blocks, lane_rows, features), 'expert', spli...  55.2 us
    all_to_all x1, blocking collectives, shards(): lax.all_to_all(row_dy.reshape(blocks, lane_rows, features), 'expert', spl...  51.5 us
    all_to_all x1, waiting for transfers between devices, shards(): lax.all_to_all(source_gu.reshape(2, devices, piece_rows, features), 'expe...  36.8 us
    all_to_all x1, waiting for transfers between devices, shards(): lax.all_to_all(helper_gu.reshape(2, devices, piece_rows, features), 'expe...  35.9 us
    all_to_all x1, waiting for transfers between devices, shards(): lax.all_to_all(spread_gu, 'expert', split_axis=1, concat_axis=1, tiled=True)  35 us
    all_to_all x1, waiting for transfers between devices, shards(): lax.all_to_all(back_gu, 'expert', split_axis=1, concat_axis=1, tiled=True)  29.9 us
    unnamed x5, waiting for transfers between devices  23.3 us
    all_to_all x1, waiting for transfers between devices, shards(): lax.all_to_all(jnp.stack(jnp.split(row_dx, lax.axis_size('expert'), axis=...  22.8 us
  transfers between devices with their start and end apart: 14, of which 11 were waited for; matrix products, arithmetic and copies ran while one was open for 9% of the time, Pallas kernels for 0%

profile of v1, /device:TPU:0, one launch (start us, length us, event | category | flops | bytes accessed | tf_op | source)
XLA Modules:
  0.0 528.3 jit_solution(6579140861374855946)
XLA Ops:
  11.6 1.4 copy.112
  13.0 55.2 %all_to_all.73 = bf16[3,128,2048]{2,0,1:T(4,128)(2,1)S(1)} all-to-all(bf16[3,128,2048]{2,0,1:T(4,128)(2,1)S(1)} %copy.112), channel_id=1, replica_groups=mesh['dp'=4,'expert'=8] {'expert'}, dimensions={1} | all-to-all | bytes 3145728 | tf_op jit(solution)/shard_map/all_to_all | solution.py:93
  68.2 2.3 copy.113
  71.1 1.4 copy.110
  72.5 51.5 %all_to_all.74 = bf16[3,128,2048]{2,0,1:T(4,128)(2,1)S(1)} all-to-all(bf16[3,128,2048]{2,0,1:T(4,128)(2,1)S(1)} %copy.110), channel_id=1, replica_groups=mesh['dp'=4,'expert'=8] {'expert'}, dimensions={1} | all-to-all | bytes 3145728 | tf_op jit(solution)/shard_map/all_to_all | solution.py:100
  124.0 2.3 copy.111
  129.1 1.3 copy.115
  130.3 3.7 all-to-all-start.5
  134.1 0.9 constant_dynamic-slice_fusion.1
  135.0 36.8 %all-to-all-done.5 = bf16[2,8,24,2048]{3,2,0,1:T(8,128)(2,1)S(1)} async-done(((bf16[2,8,24,2048]{3,2,0,1:T(8,128)(2,1)}), bf16[2,8,24,2048]{3,2,0,1:T(8,128)(2,1)S(1)}, u32[]{:S(2)}, u32[]{:S(2)}) %all-to-all-start.5) | async-done | bytes 1572896 | tf_op jit(solution)/shard_map/all_to_all | solution.py:127
  171.8 4.2 all-to-all-start.3
  176.8 1.4 select_bitcast_fusion.1
  178.2 18.7 %all-to-all-done.3 = bf16[1,8,24,2048]{3,2,0,1:T(8,128)(2,1)} async-done(((bf16[1,8,24,2048]{3,2,0,1:T(8,128)(2,1)}), bf16[1,8,24,2048]{3,2,0,1:T(8,128)(2,1)}, u32[]{:S(2)}, u32[]{:S(2)}) %all-to-all-start.3) | async-done | bytes 786464 | tf_op jit(solution)/shard_map/all_to_all | solution.py:134
  196.9 3.6 all-to-all-start.6
  200.5 1.7 gather_fusion
  202.3 1.0 fusion.42
  203.3 35.0 %all-to-all-done.6 = bf16[2,8,24,2048]{3,2,0,1:T(8,128)(2,1)S(1)} async-done(((bf16[2,8,24,2048]{3,2,0,1:T(8,128)(2,1)}), bf16[2,8,24,2048]{3,2,0,1:T(8,128)(2,1)S(1)}, u32[]{:S(2)}, u32[]{:S(2)}) %all-to-all-start.6) | async-done | bytes 1572896 | tf_op jit(solution)/shard_map/all_to_all | solution.py:145
  238.3 4.2 all-to-all-start.4
  242.9 2.6 fusion.34
  245.7 17.8 %all-to-all-done.4 = bf16[1,8,24,2048]{3,2,0,1:T(8,128)(2,1)} async-done(((bf16[1,8,24,2048]{3,2,0,1:T(8,128)(2,1)}), bf16[1,8,24,2048]{3,2,0,1:T(8,128)(2,1)}, u32[]{:S(2)}, u32[]{:S(2)}) %all-to-all-start.4) | async-done | bytes 786464 | tf_op jit(solution)/shard_map/all_to_all | solution.py:146
  263.4 2.8 fusion.8
  266.3 3.2 fusion.35
  271.4 1.1 copy-done.6
  272.5 2.6 fusion.38
  277.0 23.2 %reduce-scatter.7.cloned.1.call-done = bf16[128,3]{1,0:T(8,128)(2,1)} async-done(((bf16[512,3]{1,0:T(8,128)(2,1)}), bf16[128,3]{1,0:T(8,128)(2,1)}) %reduce-scatter.7.cloned.1.call-update) | async-done | bytes 784
  300.2 1.5 copy.119
  301.7 4.6 all-to-all-start.8
  306.4 5.5 %all-to-all-done.8 = bf16[3,8,16]{2,0,1:T(4,128)(2,1)S(1)} async-done(((bf16[3,8,16]{2,0,1:T(4,128)(2,1)}), bf16[3,8,16]{2,0,1:T(4,128)(2,1)S(1)}, u32[]{:S(2)}, u32[]{:S(2)}) %all-to-all-start.8) | async-done | bytes 800 | tf_op jit(solution)/shard_map/all_to_all | solution.py:209
  312.3 8.0 %all_to_all.75 = bf16[3,8,16]{2,0,1:T(4,128)(2,1)S(1)} all-to-all(bf16[3,8,16]{2,0,1:T(4,128)(2,1)S(1)} %copy.108), channel_id=1, replica_groups=mesh['dp'=4,'expert'=8] {'expert'}, dimensions={1} | all-to-all | bytes 1536 | tf_op jit(solution)/shard_map/all_to_all | solution.py:107
  320.4 8.2 %all_gather.9 = bf16[3,512]{1,0:T(4,128)(2,1)S(1)} all-gather(bf16[3,128]{1,0:T(4,128)(2,1)S(1)} %all_to_all.46), channel_id=1, replica_groups=mesh['dp'=4,'expert'=8] {'dp'}, dimensions={1}, use_global_device_ids=true | all-gather | bytes 3840 | tf_op jit(solution)/shard_map/all_gather | solution.py:114
  328.6 2.9 fusion.107
  331.6 1.3 fusion.13
  334.0 1.0 fusion.106
  335.9 1.3 fusion.12
  337.2 1.0 fusion.105
  338.2 1.3 fusion.11
  339.5 3.3 pad_maximum_fusion
  343.7 3.2 convolution_convert_fusion.3
  347.0 3.5 all-to-all-start.11
  350.6 2.6 convolution_convert_fusion.2
  353.1 1.2 copy.121
  354.4 17.0 %all-to-all-done.11 = bf16[1,8,24,2048]{3,2,0,1:T(8,128)(2,1)S(1)} async-done(((bf16[1,8,24,2048]{3,2,0,1:T(8,128)(2,1)}), bf16[1,8,24,2048]{3,2,0,1:T(8,128)(2,1)S(1)}, u32[]{:S(2)}, u32[]{:S(2)}) %all-to-all-start.11) | async-done | bytes 786464 | tf_op jit(solution)/shard_map/all_to_all | solution.py:178
  371.4 3.6 all-to-all-start.9
  375.7 1.0 fusion.41
  376.8 35.9 %all-to-all-done.9 = bf16[2,8,24,2048]{3,2,0,1:T(8,128)(2,1)S(1)} async-done(((bf16[2,8,24,2048]{3,2,0,1:T(8,128)(2,1)}), bf16[2,8,24,2048]{3,2,0,1:T(8,128)(2,1)S(1)}, u32[]{:S(2)}, u32[]{:S(2)}) %all-to-all-start.9) | async-done | bytes 1572896 | tf_op jit(solution)/shard_map/all_to_all | solution.py:171
  412.7 4.2 all-to-all-start.12
  419.7 1.4 select_bitcast_fusion
  422.0 15.9 %all-to-all-done.12 = bf16[1,8,24,2048]{3,2,0,1:T(8,128)(2,1)} async-done(((bf16[1,8,24,2048]{3,2,0,1:T(8,128)(2,1)}), bf16[1,8,24,2048]{3,2,0,1:T(8,128)(2,1)}, u32[]{:S(2)}, u32[]{:S(2)}) %all-to-all-start.12) | async-done | bytes 786464 | tf_op jit(solution)/shard_map/all_to_all | solution.py:190
  437.9 3.6 all-to-all-start.10
  441.5 0.9 fusion.94
  442.4 0.9 fusion.93
  444.3 0.9 fusion.91
  448.1 1.1 copy-done.2
  449.3 29.9 %all-to-all-done.10 = bf16[2,8,24,2048]{3,2,0,1:T(8,128)(2,1)S(1)} async-done(((bf16[2,8,24,2048]{3,2,0,1:T(8,128)(2,1)}), bf16[2,8,24,2048]{3,2,0,1:T(8,128)(2,1)S(1)}, u32[]{:S(2)}, u32[]{:S(2)}) %all-to-all-start.10) | async-done | bytes 1572896 | tf_op jit(solution)/shard_map/all_to_all | solution.py:189
  479.2 3.8 all-to-all-start.7
  483.1 1.5 convert_multiply_fusion.6
  484.6 2.4 fusion.18
  487.0 2.3 fusion.19
  489.3 1.3 pad_maximum_fusion.2
  493.7 1.0 fusion.15
  494.7 1.0 fusion.14
  495.7 1.9 pad_maximum_fusion.1
  497.7 22.8 %all-to-all-done.7 = bf16[8,3,16,2048]{3,2,1,0:T(8,128)(2,1)S(1)} async-done(((bf16[8,3,16,2048]{3,2,1,0:T(8,128)(2,1)}), bf16[8,3,16,2048]{3,2,1,0:T(8,128)(2,1)S(1)}, u32[]{:S(2)}, u32[]{:S(2)}) %all-to-all-start.7) | async-done | bytes 1572896 | tf_op jit(solution)/shard_map/all_to_all | solution.py:204
  520.7 1.1 convolution_convert_fusion.4
  (140 shorter events, 24.6 us)
Async XLA Ops:
  7.2 3.9 copy-start
  7.2 235.7 %all-gather.5.cloned.1.call-start = ((), (), s32[]{:S(2)}) async-start(), calls=%async_computation.16 | async-start | bytes 7864320 | tf_op jit(solution)/shard_map/all_gather | solution.py:112
  68.2 2.4 copy-start.23
  70.5 193.0 %all-gather.3.cloned.1.call-start = ((), (), s32[]{:S(2)}) async-start(), calls=%async_computation.15 | async-start | bytes 7864320 | tf_op jit(solution)/shard_map/all_gather | solution.py:113
  124.0 2.3 copy-start.25
  124.0 4.9 copy-start.5
  130.3 3.7 copy-start.10
  130.3 41.4 %all-to-all-start.5 = ((bf16[2,8,24,2048]{3,2,0,1:T(8,128)(2,1)}), bf16[2,8,24,2048]{3,2,0,1:T(8,128)(2,1)S(1)}, u32[]{:S(2)}, u32[]{:S(2)}) async-start(bf16[2,8,24,2048]{3,2,0,1:T(8,128)(2,1)} %copy.115), calls=%async_computation.5 | async-start | bytes 3145728 | tf_op jit(solution)/shard_map/all_to_all | solution.py:127
  171.8 25.2 %all-to-all-start.3 = ((bf16[1,8,24,2048]{3,2,0,1:T(8,128)(2,1)}), bf16[1,8,24,2048]{3,2,0,1:T(8,128)(2,1)}, u32[]{:S(2)}, u32[]{:S(2)}) async-start(bf16[1,8,24,2048]{3,2,0,1:T(8,128)(2,1)} %bitcast.30), calls=%async_computation.3 | async-start | bytes 1572864 | tf_op jit(solution)/shard_map/all_to_all | solution.py:134
  196.9 41.3 %all-to-all-start.6 = ((bf16[2,8,24,2048]{3,2,0,1:T(8,128)(2,1)}), bf16[2,8,24,2048]{3,2,0,1:T(8,128)(2,1)S(1)}, u32[]{:S(2)}, u32[]{:S(2)}) async-start(bf16[2,8,24,2048]{3,2,0,1:T(8,128)(2,1)} %select_bitcast_fusion.1), calls=%async_computation.6 | async-start | bytes 3145728 | tf_op jit(solution)/shard_map/all_to_all | solution.py:145
  238.3 25.2 %all-to-all-start.4 = ((bf16[1,8,24,2048]{3,2,0,1:T(8,128)(2,1)}), bf16[1,8,24,2048]{3,2,0,1:T(8,128)(2,1)}, u32[]{:S(2)}, u32[]{:S(2)}) async-start(bf16[1,8,24,2048]{3,2,0,1:T(8,128)(2,1)} %fusion.42), calls=%async_computation.4 | async-start | bytes 1572864 | tf_op jit(solution)/shard_map/all_to_all | solution.py:146
  242.5 57.7 %reduce-scatter.7.cloned.1.call-start = ((), (), s32[]{:S(2)}) async-start(), calls=%async_computation.18 | async-start | bytes 163840
  245.7 20.6 %copy-start.21 = (bf16[1,512,192]{1,2,0:T(8,128)(2,1)}, bf16[1,512,192]{1,2,0:T(8,128)(2,1)S(1)}, u32[]{:S(2)}) copy-start(bf16[1,512,192]{1,2,0:T(8,128)(2,1)S(1)} %multiply_convert_fusion) | copy-start | bytes 589828
  263.4 7.1 %slice-start.2 = ((s8[6291456]{0:T(1024)(128)(4,1)}), s8[4194304]{0:T(1024)(128)(4,1)S(1)}, s32[]{:S(2)}) async-start(s8[6291456]{0:T(1024)(128)(4,1)} %bitcast.355), calls=%async_computation.21 | async-start | bytes 8388608
  266.3 4.2 slice-start.3
  266.3 4.2 copy-start.11
  269.5 0.9 copy-start.8
  270.5 0.9 copy-start.3
  270.6 2.0 copy-start.6
  275.3 31.1 %copy-start.24 = (bf16[32,8]{0,1:T(8,128)(2,1)S(1)}, bf16[32,8]{0,1:T(8,128)(2,1)}, u32[]{:S(2)}) copy-start(bf16[32,8]{0,1:T(8,128)(2,1)} %param.16) | copy-start | bytes 1540
  301.7 10.2 %all-to-all-start.8 = ((bf16[3,8,16]{2,0,1:T(4,128)(2,1)}), bf16[3,8,16]{2,0,1:T(4,128)(2,1)S(1)}, u32[]{:S(2)}, u32[]{:S(2)}) async-start(bf16[3,8,16]{2,0,1:T(4,128)(2,1)} %copy.119), calls=%async_computation.9 | async-start | bytes 16384 | tf_op jit(solution)/shard_map/all_to_all | solution.py:209
  306.3 114.8 %reduce-scatter.5.cloned.1.call-start = ((), (), s32[]{:S(2)}) async-start(), calls=%async_computation.17 | async-start | bytes 7864320 | tf_op jit(solution)/shard_map/reduce_scatter | solution.py:197
  328.6 4.3 slice-start.4
  331.5 1.3 copy-start.26
  331.6 1.3 copy-start.28
  331.6 1.8 slice-start.5
  331.6 1.9 copy-start.9
  331.6 2.4 copy-start.12
  334.0 1.9 copy-start.7
  335.0 2.2 copy-start.13
  335.0 2.2 copy-start.15
  338.2 1.3 copy-start.17
  338.2 1.3 copy-start.19
  342.8 0.9 copy-start.22
  343.7 6.8 %copy-start.27 = (bf16[1,512,192]{1,2,0:T(8,128)(2,1)S(1)}, bf16[1,512,192]{1,2,0:T(8,128)(2,1)}, u32[]{:S(2)}) copy-start(bf16[1,512,192]{1,2,0:T(8,128)(2,1)} %copy-done.26) | copy-start | bytes 589828
  343.7 6.8 %copy-start.29 = (bf16[1,512,192]{1,2,0:T(8,128)(2,1)S(1)}, bf16[1,512,192]{1,2,0:T(8,128)(2,1)}, u32[]{:S(2)}) copy-start(bf16[1,512,192]{1,2,0:T(8,128)(2,1)} %copy-done.28) | copy-start | bytes 589828
  347.0 24.4 %all-to-all-start.11 = ((bf16[1,8,24,2048]{3,2,0,1:T(8,128)(2,1)}), bf16[1,8,24,2048]{3,2,0,1:T(8,128)(2,1)S(1)}, u32[]{:S(2)}, u32[]{:S(2)}) async-start(bf16[1,8,24,2048]{3,2,0,1:T(8,128)(2,1)} %bitcast.70), calls=%async_computation.12 | async-start | bytes 1572864 | tf_op jit(solution)/shard_map/all_to_all | solution.py:178
  371.4 41.3 %all-to-all-start.9 = ((bf16[2,8,24,2048]{3,2,0,1:T(8,128)(2,1)}), bf16[2,8,24,2048]{3,2,0,1:T(8,128)(2,1)S(1)}, u32[]{:S(2)}, u32[]{:S(2)}) async-start(bf16[2,8,24,2048]{3,2,0,1:T(8,128)(2,1)} %copy.121), calls=%async_computation.10 | async-start | bytes 3145728 | tf_op jit(solution)/shard_map/all_to_all | solution.py:171
  412.7 25.2 %all-to-all-start.12 = ((bf16[1,8,24,2048]{3,2,0,1:T(8,128)(2,1)}), bf16[1,8,24,2048]{3,2,0,1:T(8,128)(2,1)}, u32[]{:S(2)}, u32[]{:S(2)}) async-start(bf16[1,8,24,2048]{3,2,0,1:T(8,128)(2,1)} %fusion.41), calls=%async_computation.13 | async-start | bytes 1572864 | tf_op jit(solution)/shard_map/all_to_all | solution.py:190
  437.9 41.3 %all-to-all-start.10 = ((bf16[2,8,24,2048]{3,2,0,1:T(8,128)(2,1)}), bf16[2,8,24,2048]{3,2,0,1:T(8,128)(2,1)S(1)}, u32[]{:S(2)}, u32[]{:S(2)}) async-start(bf16[2,8,24,2048]{3,2,0,1:T(8,128)(2,1)} %select_bitcast_fusion), calls=%async_computation.11 | async-start | bytes 3145728 | tf_op jit(solution)/shard_map/all_to_all | solution.py:189
  448.1 1.1 copy-start.2
  479.2 41.3 %all-to-all-start.7 = ((bf16[8,3,16,2048]{3,2,1,0:T(8,128)(2,1)}), bf16[8,3,16,2048]{3,2,1,0:T(8,128)(2,1)S(1)}, u32[]{:S(2)}, u32[]{:S(2)}) async-start(bf16[8,3,16,2048]{3,2,1,0:T(8,128)(2,1)} %copy-done.2), calls=%async_computation.8 | async-start | bytes 3145728 | tf_op jit(solution)/shard_map/all_to_all | solution.py:204
  483.0 1.6 copy-start.4
  490.6 2.2 slice-start
  491.4 2.3 slice-start.1
  491.8 1.9 copy-start.14
  491.8 1.9 copy-start.16
  493.7 1.0 copy-start.18
  493.7 1.0 copy-start.20
  520.5 1.2 copy-start.1
Sparse Core Ops, SparseCore 0:
  70.6 68.9 all-gather.4
  141.4 70.0 all-gather.2
  277.1 23.0 reduce-scatter.6
  343.0 67.2 reduce-scatter.4
